TPU v7x, 32 devices: a whole 2x2x4 slice. The times are simulated.
32 devices in a mesh: rx: 4 (over z), ry: 8 (over y, x, core).
Axes of the slice: x: 2, y: 2, z: 4, core: 2. Of those that a mesh axis runs over, the one named last changes fastest.
Arguments:
- features: bfloat16 [256, 64, 512], P(('rx', 'ry')), may hold values from -6 to 6
- grad_out: bfloat16 [256, 64, 512], P(('rx', 'ry')), may hold values from -6 to 6
- weights: bfloat16 [27, 64, 64], replicated, may hold values from -0.15625 to 0.15625
- live_count: int32 [32], P(('rx', 'ry')), may hold values from 0 to 8, as said below
- neighbor: int32 [256, 6], P(('rx', 'ry')), may hold values from -1 to 23, as said below
- send_list: int32 [128, 4], P(('rx', 'ry')), may hold values from -1 to 7, as said below
Outputs:
- output: bfloat16 [256, 64, 512], P(('rx', 'ry'))
- grad_features: bfloat16 [256, 64, 512], P(('rx', 'ry'))
- grad_weights: float32 [27, 64, 64], replicated
Inputs may be any that keep to these rules, and one draw needn't show every extreme that they name: A device's occupied bricks take its first live_count slots; some device is full. `neighbor`: only live slots have entries other than -1. Entries of 8 or more stand only in columns 0 to 3, equal 8 + s * 4 + k in column s, and never point beyond the grid of devices. Sides 4 and 5 are always within the device. Adjacency is mutual: a brick is its neighbour's neighbour on the opposite side, and each received face slot of a side is used by at most one brick. `send_list`: row 4 d + t lists distinct live slots of device d, their face t going to the device beside d on side t; used entries come first, then -1.
All inputs are finite; a program needn't handle non-finite values.
Results may differ from a plain program's by a relative error of at most 0.0025.
Values may be sent and summed in bfloat16 or wider, within the bound.
A program may use at most 64 MiB of HBM per device.

v0:
```python
import functools

import jax
import jax.numpy as jnp
from jax import lax
from jax.experimental import pallas as pl
from jax.experimental.pallas import tpu as pltpu
from jax.sharding import PartitionSpec as P

MESH = pl.DeviceIdType.MESH
ROWS = 1024


def low_lanes(shape):
    return lax.broadcasted_iota(jnp.int32, shape, len(shape) - 1) < 64


def pack_kernel(live_ref, send_ref, feat_ref, grad_ref, t_ref, out_ref):
    slots = feat_ref.shape[0]

    def one(g, carry):
        both = jnp.concatenate([feat_ref[g], grad_ref[g]], axis=0).astype(jnp.float32)
        cells = jnp.transpose(both)
        cells = jnp.where(g < live_ref[0], cells, 0.0)
        t_ref[g] = cells.reshape(8, 8, 8, 128)
        return carry

    lax.fori_loop(0, slots, one, 0)
    for t in range(4):
        for k in range(send_ref.shape[1]):
            slot = send_ref[t, k]
            e = jnp.maximum(slot, 0)
            if t < 2:
                face = t_ref[e, 0 if t == 0 else 7]
            else:
                face = t_ref[e, :, 0 if t == 2 else 7]
            face = jnp.where(slot >= 0, face, 0.0)
            out_ref[t, k] = face.reshape(64, 128).astype(jnp.bfloat16)


def swap_kernel(
    n_rx, n_ry, live_ref, list_ref, feat_ref, grad_ref, w_ref,
    t_ref, recv_ref, wf_ref, wb_ref, send_ref, send_sem, recv_sem,
):
    row, col = lax.axis_index("rx"), lax.axis_index("ry")
    sides = [
        (row > 0, (row - 1, col)),
        (row < n_rx - 1, (row + 1, col)),
        (col > 0, (row, col - 1)),
        (col < n_ry - 1, (row, col + 1)),
    ]
    barrier = pltpu.get_barrier_semaphore()
    for there, peer in sides:

        @pl.when(there)
        def _():
            pl.semaphore_signal(barrier, inc=1, device_id=peer, device_id_type=MESH)

    pack_kernel(live_ref, list_ref, feat_ref, grad_ref, t_ref, send_ref)
    peers = sum(jnp.where(there, 1, 0) for there, _ in sides)
    pl.semaphore_wait(barrier, peers)

    def copy(t, into, peer):
        return pltpu.make_async_remote_copy(
            src_ref=send_ref.at[t],
            dst_ref=recv_ref.at[into],
            send_sem=send_sem.at[t],
            recv_sem=recv_sem.at[into],
            device_id=peer,
            device_id_type=MESH,
        )

    for t, (there, peer) in enumerate(sides):

        @pl.when(there)
        def _():
            copy(t, t ^ 1, peer).start()

        @pl.when(jnp.logical_not(there))
        def _():
            recv_ref[t] = jnp.zeros(recv_ref.shape[1:], recv_ref.dtype)

    gap = jnp.zeros((64, 64), jnp.float32)
    wide = jnp.zeros((64, 256), jnp.bfloat16)
    for a in range(3):
        wf_ref[a, 192:256] = wide
        wb_ref[a, 0:64] = wide
        for c in range(3):
            ahead = [w_ref[9 * a + 3 * b + c].astype(jnp.float32) for b in range(3)]
            block = jnp.transpose(jnp.concatenate(ahead + [gap], axis=0))
            wf_ref[a, 64 * c : 64 * c + 64] = block.astype(jnp.bfloat16)
            back = [w_ref[26 - 9 * a - 3 * b - c].astype(jnp.float32) for b in range(3)]
            block = jnp.concatenate([back[1], back[0], gap, back[2]], axis=1)
            at = 64 * (2, 3, 1)[c]
            wb_ref[a, at : at + 64] = block.astype(jnp.bfloat16)

    for t, (there, peer) in enumerate(sides):

        @pl.when(there)
        def _():
            copy(t, t ^ 1, peer).wait_send()
            copy(t, t, peer).wait_recv()


def conv_kernel(
    slots, nb_ref, live_ref, t_ref, recv_ref, wf_ref, wb_ref,
    out_ref, gf_ref, dw_ref, pad, under, over, xs, acc,
):
    g = pl.program_id(0)
    cap = recv_ref.shape[1]

    @pl.when(g == 0)
    def _():
        pad[...] = jnp.zeros_like(pad)
        under[...] = jnp.zeros_like(under)
        over[...] = jnp.zeros_like(over)
        acc[...] = jnp.zeros_like(acc)

    own = t_ref[g]
    pad[1:9, 1:9] = own
    for s in range(4):
        entry = nb_ref[g, s]
        e = jnp.clip(entry, 0, slots - 1)
        k = jnp.maximum(entry - slots, 0) % cap
        layer = 7 if s % 2 == 0 else 0
        local = t_ref[e, layer] if s < 2 else t_ref[e, :, layer]
        far = recv_ref[s, k].astype(jnp.float32).reshape(8, 8, 128)
        face = jnp.where(entry >= slots, far, jnp.where(entry >= 0, local, 0.0))
        if s < 2:
            pad[9 * (s % 2), 1:9] = face
        else:
            pad[1:9, 9 * (s % 2)] = face
    for s, hold in ((4, under), (5, over)):
        entry = nb_ref[g, s]
        e = jnp.clip(entry, 0, slots - 1)
        hold[1:9, 1:9] = jnp.where(entry >= 0, t_ref[e], 0.0)

    mid = pad[...].reshape(100, 8, 128)
    level = lax.broadcasted_iota(jnp.int32, mid.shape, 1)
    low = pltpu.roll(jnp.where(level == 7, under[...].reshape(mid.shape), mid), 1, 1)
    high = pltpu.roll(jnp.where(level == 0, over[...].reshape(mid.shape), mid), 7, 1)
    mid, low, high = (v.reshape(800, 128) for v in (mid, low, high))
    first = low_lanes((800, 128))
    xs[:, 0:128] = jnp.where(first, low, pltpu.roll(mid, 64, 1)).astype(jnp.bfloat16)
    xs[:, 128:256] = high.astype(jnp.bfloat16)
    xs[:, 256:384] = jnp.where(first, pltpu.roll(low, 64, 1), mid).astype(jnp.bfloat16)

    yf = jnp.dot(xs[0:640, 0:256], wf_ref[0], preferred_element_type=jnp.float32)
    yb = jnp.dot(xs[0:640, 128:384], wb_ref[0], preferred_element_type=jnp.float32)
    for a in (1, 2):
        yf += jnp.dot(
            xs[80 * a : 80 * a + 640, 0:256], wf_ref[a], preferred_element_type=jnp.float32
        )
        yb += jnp.dot(
            xs[80 * a : 80 * a + 640, 128:384], wb_ref[a], preferred_element_type=jnp.float32
        )
    yf, yb = yf.reshape(8, 10, 8, 256), yb.reshape(8, 10, 8, 256)
    half = low_lanes((8, 8, 8, 128))
    swapped = jnp.where(half, yb[:, 1:9, :, 0:128], yf[:, 1:9, :, 0:128])
    total = jnp.where(half, yf[:, 0:8, :, 0:128], yb[:, 0:8, :, 0:128])
    total += yf[:, 2:10, :, 128:256] + yb[:, 2:10, :, 128:256]
    total = total.reshape(512, 128) + pltpu.roll(swapped.reshape(512, 128), 64, 1)
    total = jnp.where(g < live_ref[0], total, 0.0)
    flat = jnp.transpose(total).astype(jnp.bfloat16)
    out_ref[0] = flat[0:64]
    gf_ref[0] = flat[64:128]

    turned = pltpu.roll(own.reshape(512, 128), 64, 1).reshape(8, 8, 8, 128)
    zero = jnp.zeros((8, 1, 8, 128), jnp.float32)
    g0 = jnp.concatenate([turned, zero, zero], axis=1)
    g1 = jnp.concatenate([zero, own, zero], axis=1)
    g2 = jnp.concatenate([zero, zero, turned], axis=1)
    g01 = jnp.where(low_lanes(g0.shape), g0, g1)
    lhs = jnp.concatenate(
        [jnp.transpose(g01.reshape(640, 128)), jnp.transpose(g2.reshape(640, 128))[0:64]], axis=0
    ).astype(jnp.bfloat16)
    for a in range(3):
        acc[192 * a : 192 * a + 192] += jnp.dot(
            lhs, xs[80 * a : 80 * a + 640, 0:256], preferred_element_type=jnp.float32
        )

    @pl.when(g == slots - 1)
    def _():
        dw_ref[0:576] = acc[:, 0:128]
        rest = jnp.concatenate([acc[320:576, 128:256], jnp.zeros((64, 128), jnp.float32)], axis=0)
        top = acc[0:320, 128:256]
        dw_ref[576:896] = jnp.where(low_lanes((320, 128)), top, pltpu.roll(rest, 64, 1))
        dw_ref[896:ROWS] = jnp.zeros((ROWS - 896, 128), jnp.float32)


def sum_kernel(
    n_rx, n_ry, scale, dw_ref, whole,
    src1, got1, src2, got2, part, send_sem, sem1, sem2, sem3, sem4,
):
    row, col = lax.axis_index("rx"), lax.axis_index("ry")
    size = dw_ref.shape[0] // n_ry
    piece = size // n_rx
    cols = [lax.rem(col + d, n_ry) for d in range(1, n_ry)]
    rows = [lax.rem(row + d, n_rx) for d in range(1, n_rx)]
    barrier = pltpu.get_barrier_semaphore()
    for c in cols:
        pl.semaphore_signal(barrier, inc=1, device_id=(row, c), device_id_type=MESH)
    for r in rows:
        pl.semaphore_signal(barrier, inc=1, device_id=(r, col), device_id_type=MESH)
    src1[...] = dw_ref[...].reshape(n_ry, size, 128)
    pl.semaphore_wait(barrier, n_ry + n_rx - 2)

    def copy(src, dst, stage, n, sem, peer):
        return pltpu.make_async_remote_copy(
            src_ref=src, dst_ref=dst, send_sem=send_sem.at[stage, n], recv_sem=sem,
            device_id=peer, device_id_type=MESH,
        )

    sent = []
    for n, c in enumerate(cols):
        x = copy(src1.at[c], got1.at[col], 0, n, sem1.at[col], (row, c))
        x.start()
        sent.append(x)
    mine = dw_ref[pl.ds(pl.multiple_of(col * size, 8), size), :]
    for n, c in enumerate(reversed(cols)):
        copy(src1.at[c], got1.at[c], 0, n, sem1.at[c], (row, c)).wait_recv()
        mine += got1[c]

    src2[...] = mine.reshape(n_rx, piece, 128)
    for n, r in enumerate(rows):
        x = copy(src2.at[r], got2.at[row], 1, n, sem2.at[row], (r, col))
        x.start()
        sent.append(x)
    small = src2[row]
    for n, r in enumerate(reversed(rows)):
        copy(src2.at[r], got2.at[r], 1, n, sem2.at[r], (r, col)).wait_recv()
        small += got2[r]

    part[row] = (small * scale).astype(part.dtype)
    for n, r in enumerate(rows):
        x = copy(part.at[row], part.at[row], 2, n, sem3.at[row], (r, col))
        x.start()
        sent.append(x)
    for n, r in enumerate(reversed(rows)):
        copy(part.at[r], part.at[r], 2, n, sem3.at[r], (r, col)).wait_recv()

    for n, c in enumerate(cols):
        x = copy(part, whole.at[col], 3, n, sem4.at[col], (row, c))
        x.start()
        sent.append(x)
    whole[col] = part[...]
    for n, c in enumerate(reversed(cols)):
        copy(part, whole.at[c], 3, n, sem4.at[c], (row, c)).wait_recv()
    for x in sent:
        x.wait_send()


def unpack_kernel(packed_ref, out_ref):
    full = packed_ref[...].astype(jnp.float32).reshape(ROWS, 128)
    for n in range(9):
        pair = full[64 * n : 64 * n + 64]
        out_ref[3 * n] = pair[:, 0:64]
        out_ref[3 * n + 1] = pair[:, 64:128]
        at, half = 576 + 64 * (n % 5), 64 * (n // 5)
        out_ref[3 * n + 2] = full[at : at + 64, half : half + 64]


def body(features, grad_out, weights, live_count, neighbor, send_list):
    slots, channels = features.shape[0], features.shape[1]
    cap = send_list.shape[1]
    n_rx, n_ry = lax.axis_size("rx"), lax.axis_size("ry")
    f32, bf16 = jnp.float32, jnp.bfloat16
    vmem = pl.BlockSpec(memory_space=pltpu.VMEM)
    smem = pl.BlockSpec(memory_space=pltpu.SMEM)

    cells, received, forward, backward = pl.pallas_call(
        functools.partial(swap_kernel, n_rx, n_ry),
        out_shape=(
            jax.ShapeDtypeStruct((slots, 8, 8, 8, 128), f32),
            jax.ShapeDtypeStruct((4, cap, 64, 128), bf16),
            jax.ShapeDtypeStruct((3, 256, 256), bf16),
            jax.ShapeDtypeStruct((3, 256, 256), bf16),
        ),
        in_specs=[smem, smem, vmem, vmem, vmem],
        out_specs=(vmem, vmem, vmem, vmem),
        scratch_shapes=[
            pltpu.VMEM((4, cap, 64, 128), bf16),
            pltpu.SemaphoreType.DMA((4,)),
            pltpu.SemaphoreType.DMA((4,)),
        ],
        compiler_params=pltpu.CompilerParams(collective_id=0, has_side_effects=True),
        name="swap",
    )(live_count, send_list, features, grad_out, weights)

    block = pl.BlockSpec((1, channels, 512), lambda g: (g, 0, 0))
    output, grad_features, dw = pl.pallas_call(
        functools.partial(conv_kernel, slots),
        grid=(slots,),
        out_shape=(
            jax.ShapeDtypeStruct(features.shape, bf16),
            jax.ShapeDtypeStruct(features.shape, bf16),
            jax.ShapeDtypeStruct((ROWS, 128), f32),
        ),
        in_specs=[smem, smem, vmem, vmem, vmem, vmem],
        out_specs=(block, block, pl.BlockSpec((ROWS, 128), lambda g: (0, 0))),
        scratch_shapes=[
            pltpu.VMEM((10, 10, 8, 128), f32),
            pltpu.VMEM((10, 10, 8, 128), f32),
            pltpu.VMEM((10, 10, 8, 128), f32),
            pltpu.VMEM((800, 384), bf16),
            pltpu.VMEM((576, 256), f32),
        ],
        name="conv",
    )(neighbor, live_count, cells, received, forward, backward)

    scale = (512.0 * slots * n_rx * n_ry) ** (-0.5)
    size = ROWS // n_ry
    piece = size // n_rx
    most = max(n_rx, n_ry)
    packed = pl.pallas_call(
        functools.partial(sum_kernel, n_rx, n_ry, scale),
        out_shape=jax.ShapeDtypeStruct((n_ry, n_rx, piece, 128), bf16),
        in_specs=[vmem],
        out_specs=vmem,
        scratch_shapes=[
            pltpu.VMEM((n_ry, size, 128), f32),
            pltpu.VMEM((n_ry, size, 128), f32),
            pltpu.VMEM((n_rx, piece, 128), f32),
            pltpu.VMEM((n_rx, piece, 128), f32),
            pltpu.VMEM((n_rx, piece, 128), bf16),
            pltpu.SemaphoreType.DMA((4, most)),
            pltpu.SemaphoreType.DMA((n_ry,)),
            pltpu.SemaphoreType.DMA((n_rx,)),
            pltpu.SemaphoreType.DMA((n_rx,)),
            pltpu.SemaphoreType.DMA((n_ry,)),
        ],
        compiler_params=pltpu.CompilerParams(collective_id=1, has_side_effects=True),
        name="total",
    )(dw)
    grad_weights = pl.pallas_call(
        unpack_kernel,
        out_shape=jax.ShapeDtypeStruct((27, channels, channels), f32),
        in_specs=[vmem],
        out_specs=vmem,
        name="unpack",
    )(packed)
    return output, grad_features, grad_weights


def solution(mesh):
    placed = (
        P(("rx", "ry"), None, None),
        P(("rx", "ry"), None, None),
        P(),
        P(("rx", "ry")),
        P(("rx", "ry"), None),
        P(("rx", "ry"), None),
    )
    return jax.shard_map(
        body,
        mesh=mesh,
        in_specs=placed,
        out_specs=(P(("rx", "ry"), None, None), P(("rx", "ry"), None, None), P()),
        check_vma=False,
    )
```

profile of v0, /device:TPU:0, one launch (start us, length us, event | category | flops | bytes accessed | tf_op | source)
XLA Modules:
  0.0 48.8 jit_solution(16618813571757295619)
XLA Ops:
  1.3 10.0 %swap.1 = (f32[8,8,8,8,128]{4,3,2,1,0:T(8,128)}, bf16[4,4,64,128]{3,2,1,0:T(8,128)(2,1)}, bf16[3,256,256]{2,1,0:T(8,128)(2,1)}, bf16[3,256,256]{2,1,0:T(8,128)(2,1)}) custom-call(s32[1]{0:T(128)S(6)} %copy.9.live_ref, s32[4,4]{1,0:T(4,128)} %list_ref.1, bf16[8,64,512]{2,1,0:T(8,128)(2,1)} %feat_ref.1, bf16[8,64,512]{2,1,0:T(8,128)(2,1)} %grad_ref.1, ...), custom_call_target="tpu_custom_call" | custom-call | tf_op jit(solution)/shard_map/swap/pallas_call | solution.py:271
  11.3 11.4 %conv.1 = (bf16[8,64,512]{2,1,0:T(8,128)(2,1)}, bf16[8,64,512]{2,1,0:T(8,128)(2,1)}, f32[1024,128]{1,0:T(8,128)}) custom-call(s32[8,6]{1,0:T(8,128)} %nb_ref.1, s32[1]{0:T(128)S(6)} %copy.9.live_ref, f32[8,8,8,8,128]{4,3,2,1,0:T(8,128)} %get-tuple-element.10.t_ref, bf16[4,4,64,128]{3,2,1,0:T(8,128)(2,1)} %get-tuple-element.11.recv_ref, ...), custom_call_target="tpu_custom_call" | custom-call | tf_op jit(solution)/shard_map/conv/pallas_call | solution.py:291
  22.7 24.1 %total.1.packed_ref = bf16[8,4,32,128]{3,2,1,0:T(8,128)(2,1)} custom-call(f32[1024,128]{1,0:T(8,128)} %get-tuple-element.16.dw_ref), custom_call_target="tpu_custom_call" | custom-call | tf_op jit(solution)/shard_map/total/pallas_call | solution.py:315
  46.9 2.0 %unpack.1 = f32[27,64,64]{2,1,0:T(8,128)} custom-call(bf16[8,4,32,128]{3,2,1,0:T(8,128)(2,1)} %total.1.packed_ref), custom_call_target="tpu_custom_call" | custom-call | tf_op jit(solution)/shard_map/unpack/pallas_call | solution.py:335
where the time goes:
time: 49.1 us; the launch traced here: 48.8 us
  Pallas kernels  47.6 us (97%)
  between operations  1.3 us (3%)
    pallas_call x1, Pallas kernels, body(): pl.pallas_call(functools.partial(sum_kernel, n_rx, n_ry, scale), out_shap...  24.1 us
    pallas_call x1, Pallas kernels, body(): pl.pallas_call(functools.partial(conv_kernel, slots), grid=(slots,), out_...  11.4 us
    pallas_call x1, Pallas kernels, body(): pl.pallas_call(functools.partial(swap_kernel, n_rx, n_ry), out_shape=(jax...  10 us
    pallas_call x1, Pallas kernels, body(): pl.pallas_call(unpack_kernel, out_shape=jax.ShapeDtypeStruct((27, channel...  1.99 us

commit v1 on v0

v1 whole, which is shorter than its diff:
```python
import functools

import jax
import jax.numpy as jnp
from jax import lax
from jax.experimental import pallas as pl
from jax.experimental.pallas import tpu as pltpu
from jax.sharding import PartitionSpec as P

MESH = pl.DeviceIdType.MESH
ROWS = 1024
F32, BF16 = jnp.float32, jnp.bfloat16


def dot(x, y):
    return jnp.dot(x, y, preferred_element_type=F32)


def low_lanes(shape):
    return lax.broadcasted_iota(jnp.int32, shape, len(shape) - 1) < 64


def put_window(ref, g, at, mid, low, high):
    rows = mid.shape[0] * 8
    mid, low, high = (v.reshape(rows, 128) for v in (mid, low, high))
    first = low_lanes((rows, 128))
    ref[g, at : at + rows, 0:128] = jnp.where(first, low, pltpu.roll(mid, 64, 1)).astype(BF16)
    ref[g, at : at + rows, 128:256] = high.astype(BF16)
    ref[g, at : at + rows, 256:384] = jnp.where(first, pltpu.roll(low, 64, 1), mid).astype(BF16)


def main_kernel(
    n_rx, n_ry, scale, conv_at,
    live_ref, list_ref, nb_ref, feat_ref, grad_ref, w_ref,
    out_ref, gf_ref, whole,
    t_ref, face_ref, recv_ref, wf_ref, wb_ref, xm_ref, xy_ref, lhs_ref, lhsx_ref, lhsf_ref, acc,
    dw, got0, src1, got1, src2, got2, part,
    face_send, face_recv, send_sem, sem0, sem1, sem2, sem3, sem4, sem5,
):
    slots = feat_ref.shape[0]
    cap = recv_ref.shape[1]
    row, col = lax.axis_index("rx"), lax.axis_index("ry")
    half, par = n_ry // 2, lax.rem(col, 2)
    me = col // 2
    partner = (row, me * 2 + 1 - par)
    others = [lax.rem(me + d, half) for d in range(1, half)]
    rows = [lax.rem(row + d, n_rx) for d in range(1, n_rx)]
    sides = [
        (row > 0, (row - 1, col)),
        (row < n_rx - 1, (row + 1, col)),
        (col > 0, (row, col - 1)),
        (col < n_ry - 1, (row, col + 1)),
    ]

    barrier = pltpu.get_barrier_semaphore()
    for d in range(1, n_ry):
        peer = (row, lax.rem(col + d, n_ry))
        pl.semaphore_signal(barrier, inc=1, device_id=peer, device_id_type=MESH)
    for r in rows:
        pl.semaphore_signal(barrier, inc=1, device_id=(r, col), device_id_type=MESH)

    def pack(g, carry):
        both = jnp.concatenate([feat_ref[g], grad_ref[g]], axis=0).astype(F32)
        cells = jnp.where(g < live_ref[0], jnp.transpose(both), 0.0)
        t_ref[g] = cells.reshape(8, 8, 8, 128)
        return carry

    lax.fori_loop(0, slots, pack, 0)
    for t in range(4):
        for k in range(cap):
            slot = list_ref[t, k]
            e = jnp.maximum(slot, 0)
            if t < 2:
                face = t_ref[e, 0 if t == 0 else 7]
            else:
                face = t_ref[e, :, 0 if t == 2 else 7]
            face = jnp.where(slot >= 0, face, 0.0)
            face_ref[t, k] = face.reshape(64, 128).astype(BF16)
    pl.semaphore_wait(barrier, n_ry + n_rx - 2)

    def copy(src, dst, ssem, rsem, peer):
        return pltpu.make_async_remote_copy(
            src_ref=src, dst_ref=dst, send_sem=ssem, recv_sem=rsem,
            device_id=peer, device_id_type=MESH,
        )

    def swap(t, into, peer):
        return copy(face_ref.at[t], recv_ref.at[into], face_send.at[t], face_recv.at[into], peer)

    for t, (there, peer) in enumerate(sides):

        @pl.when(there)
        def _():
            swap(t, t ^ 1, peer).start()

        @pl.when(jnp.logical_not(there))
        def _():
            recv_ref[t] = jnp.zeros(recv_ref.shape[1:], recv_ref.dtype)

    acc[...] = jnp.zeros_like(acc)
    xy_ref[...] = jnp.zeros_like(xy_ref)
    level = lax.broadcasted_iota(jnp.int32, (64, 8, 128), 1)

    def inner(p, carry):
        lane = lax.broadcasted_iota(jnp.int32, (64, 512), 1) % 64
        edges = []
        for h in range(2):
            g = 2 * p + h
            grads = jnp.where(g < live_ref[0], grad_ref[g].astype(F32), 0.0)

            def turned(shift):
                cut = [grads[:, 128 * q : 128 * q + 128] for q in range(4)]
                return jnp.concatenate([pltpu.roll(v, shift, 1) for v in cut], axis=1)

            ahead = jnp.where(lane < 56, turned(120), 0.0)
            behind = jnp.where(lane >= 8, turned(8), 0.0)
            lhs = jnp.concatenate([ahead, grads, behind], axis=0)
            lhs_ref[g] = lhs.astype(BF16)
            edges.append((lhs[:, 0:128], lhs[:, 384:512]))
            own = t_ref[g]
            ends = jnp.concatenate([own[:, 0:1], own[:, 7:8]], axis=1).reshape(128, 128)
            ends = jnp.transpose(ends)[64:128]
            which = lax.broadcasted_iota(jnp.int32, (64, 128), 1) % 16 < 8
            lhsf_ref[g] = jnp.concatenate(
                [jnp.where(which, ends, 0.0), jnp.where(which, 0.0, ends)], axis=0
            ).astype(BF16)

            mid = own.reshape(64, 8, 128)
            below, above = nb_ref[g, 4], nb_ref[g, 5]
            under = t_ref[jnp.clip(below, 0, slots - 1)].reshape(64, 8, 128)
            over = t_ref[jnp.clip(above, 0, slots - 1)].reshape(64, 8, 128)
            under = jnp.where(below >= 0, under, 0.0)
            over = jnp.where(above >= 0, over, 0.0)
            low = pltpu.roll(jnp.where(level == 7, under, mid), 1, 1)
            high = pltpu.roll(jnp.where(level == 0, over, mid), 7, 1)
            put_window(xm_ref, g, 64, mid, low, high)
            xm_ref[g, 0:64] = jnp.zeros((64, 384), BF16)
            xm_ref[g, 576:640] = jnp.zeros((64, 384), BF16)
            for a in range(3):
                acc[a] += dot(lhs_ref[g], xm_ref[g, 64 * a : 64 * a + 512, 0:256])
        first = low_lanes((192, 128))
        (low0, low1), (high0, high1) = edges
        lhsx_ref[0, p] = jnp.where(first, low0, pltpu.roll(high0, 64, 1)).astype(BF16)
        lhsx_ref[1, p] = jnp.where(first, pltpu.roll(low1, 64, 1), high1).astype(BF16)
        return carry

    lax.fori_loop(0, slots // 2, inner, 0)

    gap = jnp.zeros((64, 64), F32)
    wide = jnp.zeros((64, 256), BF16)
    for a in range(3):
        wf_ref[a, 192:256] = wide
        wb_ref[a, 0:64] = wide
        for c in range(3):
            front = [w_ref[9 * a + 3 * b + c].astype(F32) for b in range(3)]
            block = jnp.transpose(jnp.concatenate(front + [gap], axis=0))
            wf_ref[a, 64 * c : 64 * c + 64] = block.astype(BF16)
            back = [w_ref[26 - 9 * a - 3 * b - c].astype(F32) for b in range(3)]
            block = jnp.concatenate([back[1], back[0], gap, back[2]], axis=1)
            at = 64 * (2, 3, 1)[c]
            wb_ref[a, at : at + 64] = block.astype(BF16)

    for t, (there, peer) in enumerate(sides):

        @pl.when(there)
        def _():
            swap(t, t ^ 1, peer).wait_send()
            swap(t, t, peer).wait_recv()

    def faces(g, carry):
        got = []
        for s in range(4):
            entry = nb_ref[g, s]
            e = jnp.clip(entry, 0, slots - 1)
            k = jnp.maximum(entry - slots, 0) % cap
            layer = 7 if s % 2 == 0 else 0
            local = t_ref[e, layer] if s < 2 else t_ref[e, :, layer]
            far = recv_ref[s, k].astype(F32).reshape(8, 8, 128)
            got.append(jnp.where(entry >= slots, far, jnp.where(entry >= 0, local, 0.0)))

        def around(mid):
            at = lax.broadcasted_iota(jnp.int32, mid.shape, 1)
            low = pltpu.roll(jnp.where(at == 7, 0.0, mid), 1, 1)
            high = pltpu.roll(jnp.where(at == 0, 0.0, mid), 7, 1)
            return mid, low, high

        put_window(xm_ref, g, 0, *around(got[0]))
        put_window(xm_ref, g, 576, *around(got[1]))
        both = jnp.concatenate([got[2][:, None], got[3][:, None]], axis=1).reshape(16, 8, 128)
        put_window(xy_ref, g, 16, *around(both))
        return carry

    lax.fori_loop(0, slots, faces, 0)

    pairs = slots // 2
    for s, a, at in ((0, 0, 0), (1, 2, 576)):
        lhs = jnp.concatenate([lhsx_ref[s, p] for p in range(pairs)], axis=1)
        rhs = jnp.concatenate([xm_ref[g, at : at + 64, 0:256] for g in range(slots)], axis=0)
        acc[a] += dot(lhs, rhs)
    lhs = jnp.concatenate([lhsf_ref[g] for g in range(slots)], axis=1)
    for a in range(3):
        rhs = [xy_ref[g, 16 * a : 16 * a + 128, 0:256] for g in range(slots)]
        more = dot(lhs, jnp.concatenate(rhs, axis=0))
        acc[a, 0:64] += more[0:64]
        acc[a, 128:192] += more[64:128]

    size = ROWS // n_ry
    piece = size // n_rx
    flat = acc[...].reshape(576, 256)
    rest = jnp.concatenate([flat[320:576, 128:256], jnp.zeros((64, 128), F32)], axis=0)
    third = jnp.where(low_lanes((320, 128)), flat[0:320, 128:256], pltpu.roll(rest, 64, 1))
    flat = jnp.concatenate([flat[:, 0:128], third, jnp.zeros((ROWS - 896, 128), F32)], axis=0)
    dw[...] = flat.reshape(half, 2, size, 128)

    def conv(g, carry):
        yf = yb = zf = zb = None
        for a in range(3):
            m = xm_ref[g, 64 * a : 64 * a + 512]
            y = xy_ref[g, 16 * a : 16 * a + 128]
            new = [
                dot(m[:, 0:256], wf_ref[a]), dot(m[:, 128:384], wb_ref[a]),
                dot(y[:, 0:256], wf_ref[a]), dot(y[:, 128:384], wb_ref[a]),
            ]
            if a:
                yf, yb, zf, zb = yf + new[0], yb + new[1], zf + new[2], zb + new[3]
            else:
                yf, yb, zf, zb = new
        yf, yb = yf.reshape(8, 8, 8, 256), yb.reshape(8, 8, 8, 256)
        zf, zb = zf.reshape(8, 2, 8, 256), zb.reshape(8, 2, 8, 256)

        def before(y, z):
            return jnp.concatenate([z[:, 0:1, :, 0:128], y[:, 0:7, :, 0:128]], axis=1)

        def after(y, z):
            return jnp.concatenate([y[:, 1:8, :, 128:256], z[:, 1:2, :, 128:256]], axis=1)

        first = low_lanes((8, 8, 8, 128))
        swapped = jnp.where(first, yb[..., 0:128], yf[..., 0:128])
        total = jnp.where(first, before(yf, zf), before(yb, zb))
        total += after(yf, zf) + after(yb, zb)
        total = total.reshape(512, 128) + pltpu.roll(swapped.reshape(512, 128), 64, 1)
        total = jnp.where(g < live_ref[0], total, 0.0)
        flat = jnp.transpose(total).astype(BF16)
        out_ref[g] = flat[0:64]
        gf_ref[g] = flat[64:128]
        return carry

    def run(n):
        lo, hi = conv_at[n], conv_at[n + 1]
        if hi > lo:
            lax.fori_loop(lo, hi, conv, 0)

    sent = []

    def send(src, dst, stage, n, rsem, peer):
        x = copy(src, dst, send_sem.at[stage, n], rsem, peer)
        x.start()
        sent.append(x)

    def arrived(src, dst, stage, n, rsem, peer):
        copy(src, dst, send_sem.at[stage, n], rsem, peer).wait_recv()

    order = others + [me]
    for n, c in enumerate(order):
        send(dw.at[c, 1 - par], got0.at[c], 0, n, sem0.at[c], partner)
    run(0)
    for n, c in enumerate(order):
        arrived(dw.at[c, 1 - par], got0.at[c], 0, n, sem0.at[c], partner)
        src1[c] = dw[c, par] + got0[c]
        if n < half - 1:
            send(src1.at[c], got1.at[me], 1, n, sem1.at[me], (row, 2 * c + par))
    run(1)
    mine = src1[me]
    for n, c in enumerate(reversed(others)):
        arrived(src1.at[c], got1.at[c], 1, n, sem1.at[c], (row, 2 * c + par))
        mine += got1[c]
    src2[...] = mine.reshape(n_rx, piece, 128)
    for n, r in enumerate(rows):
        send(src2.at[r], got2.at[row], 2, n, sem2.at[row], (r, col))
    run(2)
    small = src2[row]
    for n, r in enumerate(reversed(rows)):
        arrived(src2.at[r], got2.at[r], 2, n, sem2.at[r], (r, col))
        small += got2[r]

    part[row] = (small * scale).astype(part.dtype)
    for n, r in enumerate(rows):
        send(part.at[row], part.at[row], 3, n, sem3.at[row], (r, col))
    run(3)
    for n, r in enumerate(reversed(rows)):
        arrived(part.at[r], part.at[r], 3, n, sem3.at[r], (r, col))
    for n, c in enumerate(others):
        send(part, whole.at[me, par], 4, n, sem4.at[me], (row, 2 * c + par))
    send(part, whole.at[me, par], 5, half - 1, sem5.at[me], partner)
    whole[me, par] = part[...]
    run(4)
    for n, c in enumerate(reversed(others)):
        arrived(part, whole.at[c, par], 4, n, sem4.at[c], (row, 2 * c + par))
        send(whole.at[c, par], whole.at[c, par], 5, n, sem5.at[c], partner)
    run(5)
    for n, c in enumerate(order):
        arrived(part, whole.at[c, 1 - par], 5, n, sem5.at[c], partner)
    for x in sent:
        x.wait_send()


def finish_kernel(packed_ref, out_ref, gf_ref, dw_ref, out, gf):
    full = packed_ref[...].astype(F32).reshape(ROWS, 128)
    for n in range(9):
        pair = full[64 * n : 64 * n + 64]
        dw_ref[3 * n] = pair[:, 0:64]
        dw_ref[3 * n + 1] = pair[:, 64:128]
        at, half = 576 + 64 * (n % 5), 64 * (n // 5)
        dw_ref[3 * n + 2] = full[at : at + 64, half : half + 64]
    out[...] = out_ref[...]
    gf[...] = gf_ref[...]


def body(features, grad_out, weights, live_count, neighbor, send_list):
    slots, channels = features.shape[0], features.shape[1]
    cap = send_list.shape[1]
    n_rx, n_ry = lax.axis_size("rx"), lax.axis_size("ry")
    vmem = pl.BlockSpec(memory_space=pltpu.VMEM)
    smem = pl.BlockSpec(memory_space=pltpu.SMEM)
    scale = (512.0 * slots * n_rx * n_ry) ** (-0.5)
    size = ROWS // n_ry
    piece = size // n_rx
    half = n_ry // 2
    most = max(n_rx, half)
    dma = pltpu.SemaphoreType.DMA
    conv_at = [n * slots // 8 for n in (0, 1, 4, 6, 7, 8, 8)]

    output, grad_features, packed = pl.pallas_call(
        functools.partial(main_kernel, n_rx, n_ry, scale, conv_at),
        out_shape=(
            jax.ShapeDtypeStruct(features.shape, BF16),
            jax.ShapeDtypeStruct(features.shape, BF16),
            jax.ShapeDtypeStruct((half, 2, n_rx, piece, 128), BF16),
        ),
        in_specs=[smem, smem, smem, vmem, vmem, vmem],
        out_specs=(vmem, vmem, vmem),
        scratch_shapes=[
            pltpu.VMEM((slots, 8, 8, 8, 128), F32),
            pltpu.VMEM((4, cap, 64, 128), BF16),
            pltpu.VMEM((4, cap, 64, 128), BF16),
            pltpu.VMEM((3, 256, 256), BF16),
            pltpu.VMEM((3, 256, 256), BF16),
            pltpu.VMEM((slots, 640, 384), BF16),
            pltpu.VMEM((slots, 160, 384), BF16),
            pltpu.VMEM((slots, 192, 512), BF16),
            pltpu.VMEM((2, slots // 2, 192, 128), BF16),
            pltpu.VMEM((slots, 128, 128), BF16),
            pltpu.VMEM((3, 192, 256), F32),
            pltpu.VMEM((half, 2, size, 128), F32),
            pltpu.VMEM((half, size, 128), F32),
            pltpu.VMEM((half, size, 128), F32),
            pltpu.VMEM((half, size, 128), F32),
            pltpu.VMEM((n_rx, piece, 128), F32),
            pltpu.VMEM((n_rx, piece, 128), F32),
            pltpu.VMEM((n_rx, piece, 128), BF16),
            dma((4,)), dma((4,)), dma((6, most)),
            dma((half,)), dma((half,)), dma((n_rx,)), dma((n_rx,)), dma((half,)), dma((half,)),
        ],
        compiler_params=pltpu.CompilerParams(collective_id=0, has_side_effects=True),
        name="main",
    )(live_count, send_list, neighbor, features, grad_out, weights)

    grad_weights, output, grad_features = pl.pallas_call(
        finish_kernel,
        out_shape=(
            jax.ShapeDtypeStruct((27, channels, channels), F32),
            jax.ShapeDtypeStruct(features.shape, BF16),
            jax.ShapeDtypeStruct(features.shape, BF16),
        ),
        in_specs=[vmem, vmem, vmem],
        out_specs=(vmem, vmem, vmem),
        name="finish",
    )(packed, output, grad_features)
    return output, grad_features, grad_weights


def solution(mesh):
    placed = (
        P(("rx", "ry"), None, None),
        P(("rx", "ry"), None, None),
        P(),
        P(("rx", "ry")),
        P(("rx", "ry"), None),
        P(("rx", "ry"), None),
    )
    return jax.shard_map(
        body,
        mesh=mesh,
        in_specs=placed,
        out_specs=(P(("rx", "ry"), None, None), P(("rx", "ry"), None, None), P()),
        check_vma=False,
    )
```

time: 49.1 us -> 35.4 us (0.72)
  Pallas kernels: 47.6 us -> 34 us
    pallas_call x4 -> x2, Pallas kernels: 47.6 us -> 34 us  [the longest x1 31.4 us: body(): pl.pallas_call(functools.partial(main_kernel, n_rx, n_ry, scale, conv_at)...]
where the time goes in v1:
time: 35.4 us; the launch traced here: 35.3 us
  Pallas kernels  34 us (96%)
  between operations  1.29 us (4%)
    pallas_call x1, Pallas kernels, body(): pl.pallas_call(functools.partial(main_kernel, n_rx, n_ry, scale, conv_at)...  31.4 us
    pallas_call x1, Pallas kernels, body(): pl.pallas_call(finish_kernel, out_shape=(jax.ShapeDtypeStruct((27, channe...  2.61 us

profile of v1, /device:TPU:0, one launch (start us, length us, event | category | flops | bytes accessed | tf_op | source)
XLA Modules:
  0.0 35.3 jit_solution(16429071257950091890)
XLA Ops:
  1.3 31.4 %main.1 = (bf16[8,64,512]{2,1,0:T(8,128)(2,1)}, bf16[8,64,512]{2,1,0:T(8,128)(2,1)}, bf16[4,2,4,32,128]{4,3,2,1,0:T(8,128)(2,1)}) custom-call(s32[1]{0:T(128)S(6)} %copy.9.live_ref, s32[4,4]{1,0:T(4,128)} %list_ref.1, s32[8,6]{1,0:T(8,128)} %nb_ref.1, bf16[8,64,512]{2,1,0:T(8,128)(2,1)} %feat_ref.1, bf16[8,64,512]{2,1,0:T(8,128)(2,1)} %grad_ref.1, ...), custom_call_target="tpu_custom_call" | custom-call | tf_op jit(solution)/shard_map/main/pallas_call | solution.py:333
  32.7 2.6 %finish.1 = (f32[27,64,64]{2,1,0:T(8,128)}, bf16[8,64,512]{2,1,0:T(8,128)(2,1)}, bf16[8,64,512]{2,1,0:T(8,128)(2,1)}) custom-call(bf16[4,2,4,32,128]{4,3,2,1,0:T(8,128)(2,1)} %get-tuple-element.9.packed_ref, bf16[8,64,512]{2,1,0:T(8,128)(2,1)} %get-tuple-element.10.out_ref, bf16[8,64,512]{2,1,0:T(8,128)(2,1)} %get-tuple-element.11.gf_ref), custom_call_target="tpu_custom_call" | custom-call | tf_op jit(solution)/shard_map/finish/pallas_call | solution.py:368

commit v2 on v1

--- a/solution.py
+++ b/solution.py
@@ -8,7 +8,6 @@
 from jax.sharding import PartitionSpec as P
 
 MESH = pl.DeviceIdType.MESH
-ROWS = 1024
 F32, BF16 = jnp.float32, jnp.bfloat16
 
 
@@ -31,14 +30,28 @@
 
 def main_kernel(
     n_rx, n_ry, scale, conv_at,
-    live_ref, list_ref, nb_ref, feat_ref, grad_ref, w_ref,
+    live_hbm, list_hbm, nb_hbm, feat_hbm, grad_hbm, w_hbm,
     out_ref, gf_ref, whole,
+    live_ref, list_ref, nb_ref, feat_ref, grad_ref, w_ref, load_sem,
     t_ref, face_ref, recv_ref, wf_ref, wb_ref, xm_ref, xy_ref, lhs_ref, lhsx_ref, lhsf_ref, acc,
-    dw, got0, src1, got1, src2, got2, part,
-    face_send, face_recv, send_sem, sem0, sem1, sem2, sem3, sem4, sem5,
+    dw, got0, src1, got1, src2, got2,
+    face_send, face_recv, send0, send1, send2, send3, send4, send5,
+    sem0, sem1, sem2, sem3, sem4, sem5,
 ):
     slots = feat_ref.shape[0]
     cap = recv_ref.shape[1]
+    total_rows = dw.shape[0] * dw.shape[1] * dw.shape[2] * dw.shape[3]
+    loads = [
+        pltpu.make_async_copy(src, dst, load_sem.at[n])
+        for n, (src, dst) in enumerate(
+            (
+                (feat_hbm, feat_ref), (grad_hbm, grad_ref), (live_hbm, live_ref),
+                (list_hbm, list_ref), (nb_hbm, nb_ref), (w_hbm, w_ref),
+            )
+        )
+    ]
+    for x in loads:
+        x.start()
     row, col = lax.axis_index("rx"), lax.axis_index("ry")
     half, par = n_ry // 2, lax.rem(col, 2)
     me = col // 2
@@ -58,6 +71,9 @@
         pl.semaphore_signal(barrier, inc=1, device_id=peer, device_id_type=MESH)
     for r in rows:
         pl.semaphore_signal(barrier, inc=1, device_id=(r, col), device_id_type=MESH)
+
+    for x in loads[:5]:
+        x.wait()
 
     def pack(g, carry):
         both = jnp.concatenate([feat_ref[g], grad_ref[g]], axis=0).astype(F32)
@@ -146,20 +162,6 @@
 
     lax.fori_loop(0, slots // 2, inner, 0)
 
-    gap = jnp.zeros((64, 64), F32)
-    wide = jnp.zeros((64, 256), BF16)
-    for a in range(3):
-        wf_ref[a, 192:256] = wide
-        wb_ref[a, 0:64] = wide
-        for c in range(3):
-            front = [w_ref[9 * a + 3 * b + c].astype(F32) for b in range(3)]
-            block = jnp.transpose(jnp.concatenate(front + [gap], axis=0))
-            wf_ref[a, 64 * c : 64 * c + 64] = block.astype(BF16)
-            back = [w_ref[26 - 9 * a - 3 * b - c].astype(F32) for b in range(3)]
-            block = jnp.concatenate([back[1], back[0], gap, back[2]], axis=1)
-            at = 64 * (2, 3, 1)[c]
-            wb_ref[a, at : at + 64] = block.astype(BF16)
-
     for t, (there, peer) in enumerate(sides):
 
         @pl.when(there)
@@ -204,13 +206,13 @@
         acc[a, 0:64] += more[0:64]
         acc[a, 128:192] += more[64:128]
 
-    size = ROWS // n_ry
-    piece = size // n_rx
     flat = acc[...].reshape(576, 256)
     rest = jnp.concatenate([flat[320:576, 128:256], jnp.zeros((64, 128), F32)], axis=0)
     third = jnp.where(low_lanes((320, 128)), flat[0:320, 128:256], pltpu.roll(rest, 64, 1))
-    flat = jnp.concatenate([flat[:, 0:128], third, jnp.zeros((ROWS - 896, 128), F32)], axis=0)
-    dw[...] = flat.reshape(half, 2, size, 128)
+    flat = [flat[:, 0:128], third]
+    if total_rows > 896:
+        flat.append(jnp.zeros((total_rows - 896, 128), F32))
+    dw[...] = jnp.concatenate(flat, axis=0).reshape(dw.shape)
 
     def conv(g, carry):
         yf = yb = zf = zb = None
@@ -250,70 +252,153 @@
         if hi > lo:
             lax.fori_loop(lo, hi, conv, 0)
 
-    sent = []
-
-    def send(src, dst, stage, n, rsem, peer):
-        x = copy(src, dst, send_sem.at[stage, n], rsem, peer)
+    mid_rows = (n_rx // 2 - 1, n_rx // 2)
+    far = jnp.where(row <= mid_rows[0], 1, 0)
+    near = 1 - far
+    row_of = {0: jnp.where(far == 1, mid_rows[1], mid_rows[0])}
+    row_of[1] = mid_rows[0] + mid_rows[1] - row_of[0]
+    share = (far, near)
+
+    def pair(h):
+        return copy(dw.at[h, 1 - par], got0.at[h], send0.at[h], sem0.at[h], partner)
+
+    def along(h, c, into):
+        peer = (row, 2 * c + par)
+        return copy(src1.at[h, c], got1.at[h, into], send1.at[h, c], sem1.at[h, into], peer)
+
+    def gather(n, source):
+        return copy(src2.at[n], got2.at[source], send2.at[n], sem2.at[source], (row_of[n], col))
+
+    def spread(h, r):
+        at = whole.at[h, par, me]
+        return copy(at, at, send3.at[r], sem3.at[h], (r, col))
+
+    def fan(h, c, m):
+        at = whole.at[h, par, m]
+        return copy(at, at, send4.at[h, c], sem4.at[h, m], (row, 2 * c + par))
+
+    def cross(h, m, parity):
+        at = whole.at[h, parity, m]
+        return copy(at, at, send5.at[h, m], sem5.at[h, m], partner)
+
+    for h in share:
+        pair(h).start()
+    loads[5].wait()
+    gap = jnp.zeros((64, 64), F32)
+    wide = jnp.zeros((64, 256), BF16)
+    for a in range(3):
+        wf_ref[a, 192:256] = wide
+        wb_ref[a, 0:64] = wide
+        for c in range(3):
+            front = [w_ref[9 * a + 3 * b + c].astype(F32) for b in range(3)]
+            block = jnp.transpose(jnp.concatenate(front + [gap], axis=0))
+            wf_ref[a, 64 * c : 64 * c + 64] = block.astype(BF16)
+            back = [w_ref[26 - 9 * a - 3 * b - c].astype(F32) for b in range(3)]
+            block = jnp.concatenate([back[1], back[0], gap, back[2]], axis=1)
+            at = 64 * (2, 3, 1)[c]
+            wb_ref[a, at : at + 64] = block.astype(BF16)
+    run(0)
+    for h in share:
+        pair(h).wait_recv()
+        src1[h] = dw[h, par] + got0[h]
+        for c in others:
+            along(h, c, me).start()
+    for n, h in enumerate(share):
+        run(1 + n)
+        mine = src1[h, me]
+        for c in reversed(others):
+            along(h, c, c).wait_recv()
+            mine += got1[h, c]
+        src2[n] = mine
+        if n == 0:
+            gather(0, row).start()
+    owner = row == row_of[1]
+
+    @pl.when(jnp.logical_not(owner))
+    def _():
+        gather(1, row).start()
+
+    run(3)
+
+    @pl.when(owner)
+    def _():
+        mine = src2[1]
+        for r in reversed(rows):
+            gather(1, r).wait_recv()
+            mine += got2[r]
+        whole[near, par, me] = (mine * scale).astype(whole.dtype)
+        for r in rows:
+            spread(near, r).start()
+
+    @pl.when(jnp.logical_not(owner))
+    def _():
+        spread(near, row).wait_recv()
+
+    def onward(h):
+        for c in others:
+            fan(h, c, me).start()
+        cross(h, me, par).start()
+
+    onward(near)
+    run(4)
+    spread(far, row).wait_recv()
+    onward(far)
+    run(5)
+    for h in (near, far):
+        for c in reversed(others):
+            fan(h, c, c).wait_recv()
+            cross(h, c, par).start()
+    for h in (near, far):
+        for c in [me] + others:
+            cross(h, c, 1 - par).wait_recv()
+
+    for n, h in enumerate(share):
+        pair(h).wait_send()
+        for c in others:
+            along(h, c, me).wait_send()
+            fan(h, c, me).wait_send()
+            cross(h, c, par).wait_send()
+        cross(h, me, par).wait_send()
+    gather(0, row).wait_send()
+
+    @pl.when(jnp.logical_not(owner))
+    def _():
+        gather(1, row).wait_send()
+
+    @pl.when(owner)
+    def _():
+        for r in rows:
+            spread(near, r).wait_send()
+
+
+def finish_kernel(packed_ref, out_ref, gf_ref, dw_hbm, out_hbm, gf_hbm, dw_ref, sem):
+    copies = [
+        pltpu.make_async_copy(out_ref, out_hbm, sem.at[0]),
+        pltpu.make_async_copy(gf_ref, gf_hbm, sem.at[1]),
+    ]
+    for x in copies:
         x.start()
-        sent.append(x)
-
-    def arrived(src, dst, stage, n, rsem, peer):
-        copy(src, dst, send_sem.at[stage, n], rsem, peer).wait_recv()
-
-    order = others + [me]
-    for n, c in enumerate(order):
-        send(dw.at[c, 1 - par], got0.at[c], 0, n, sem0.at[c], partner)
-    run(0)
-    for n, c in enumerate(order):
-        arrived(dw.at[c, 1 - par], got0.at[c], 0, n, sem0.at[c], partner)
-        src1[c] = dw[c, par] + got0[c]
-        if n < half - 1:
-            send(src1.at[c], got1.at[me], 1, n, sem1.at[me], (row, 2 * c + par))
-    run(1)
-    mine = src1[me]
-    for n, c in enumerate(reversed(others)):
-        arrived(src1.at[c], got1.at[c], 1, n, sem1.at[c], (row, 2 * c + par))
-        mine += got1[c]
-    src2[...] = mine.reshape(n_rx, piece, 128)
-    for n, r in enumerate(rows):
-        send(src2.at[r], got2.at[row], 2, n, sem2.at[row], (r, col))
-    run(2)
-    small = src2[row]
-    for n, r in enumerate(reversed(rows)):
-        arrived(src2.at[r], got2.at[r], 2, n, sem2.at[r], (r, col))
-        small += got2[r]
-
-    part[row] = (small * scale).astype(part.dtype)
-    for n, r in enumerate(rows):
-        send(part.at[row], part.at[row], 3, n, sem3.at[row], (r, col))
-    run(3)
-    for n, r in enumerate(reversed(rows)):
-        arrived(part.at[r], part.at[r], 3, n, sem3.at[r], (r, col))
-    for n, c in enumerate(others):
-        send(part, whole.at[me, par], 4, n, sem4.at[me], (row, 2 * c + par))
-    send(part, whole.at[me, par], 5, half - 1, sem5.at[me], partner)
-    whole[me, par] = part[...]
-    run(4)
-    for n, c in enumerate(reversed(others)):
-        arrived(part, whole.at[c, par], 4, n, sem4.at[c], (row, 2 * c + par))
-        send(whole.at[c, par], whole.at[c, par], 5, n, sem5.at[c], partner)
-    run(5)
-    for n, c in enumerate(order):
-        arrived(part, whole.at[c, 1 - par], 5, n, sem5.at[c], partner)
-    for x in sent:
-        x.wait_send()
-
-
-def finish_kernel(packed_ref, out_ref, gf_ref, dw_ref, out, gf):
-    full = packed_ref[...].astype(F32).reshape(ROWS, 128)
+    count = 1
+    for extent in packed_ref.shape[:-1]:
+        count *= extent
+    full = packed_ref[...].astype(F32).reshape(count, 128)
     for n in range(9):
         pair = full[64 * n : 64 * n + 64]
         dw_ref[3 * n] = pair[:, 0:64]
         dw_ref[3 * n + 1] = pair[:, 64:128]
         at, half = 576 + 64 * (n % 5), 64 * (n // 5)
         dw_ref[3 * n + 2] = full[at : at + 64, half : half + 64]
-    out[...] = out_ref[...]
-    gf[...] = gf_ref[...]
+        if n % 3 == 2:
+            done = pl.ds(3 * n - 6, 9)
+            x = pltpu.make_async_copy(dw_ref.at[done], dw_hbm.at[done], sem.at[2 + n // 3])
+            x.start()
+            copies.append(x)
+    for x in copies:
+        x.wait()
+
+
+def held(x):
+    return pltpu.with_memory_space_constraint(x, pltpu.MemorySpace.HBM)
 
 
 def body(features, grad_out, weights, live_count, neighbor, send_list):
@@ -321,25 +406,30 @@
     cap = send_list.shape[1]
     n_rx, n_ry = lax.axis_size("rx"), lax.axis_size("ry")
     vmem = pl.BlockSpec(memory_space=pltpu.VMEM)
-    smem = pl.BlockSpec(memory_space=pltpu.SMEM)
+    hbm = pl.BlockSpec(memory_space=pltpu.MemorySpace.HBM)
     scale = (512.0 * slots * n_rx * n_ry) ** (-0.5)
-    size = ROWS // n_ry
-    piece = size // n_rx
     half = n_ry // 2
-    most = max(n_rx, half)
+    unit = -(-896 // (n_ry * 16)) * 8
     dma = pltpu.SemaphoreType.DMA
-    conv_at = [n * slots // 8 for n in (0, 1, 4, 6, 7, 8, 8)]
+    conv_at = [n * slots // 8 for n in (0, 0, 4, 5, 7, 8, 8)]
 
     output, grad_features, packed = pl.pallas_call(
         functools.partial(main_kernel, n_rx, n_ry, scale, conv_at),
         out_shape=(
             jax.ShapeDtypeStruct(features.shape, BF16),
             jax.ShapeDtypeStruct(features.shape, BF16),
-            jax.ShapeDtypeStruct((half, 2, n_rx, piece, 128), BF16),
+            jax.ShapeDtypeStruct((2, 2, half, unit, 128), BF16),
         ),
-        in_specs=[smem, smem, smem, vmem, vmem, vmem],
+        in_specs=[hbm] * 6,
         out_specs=(vmem, vmem, vmem),
         scratch_shapes=[
+            pltpu.SMEM(live_count.shape, jnp.int32),
+            pltpu.SMEM(send_list.shape, jnp.int32),
+            pltpu.SMEM(neighbor.shape, jnp.int32),
+            pltpu.VMEM(features.shape, BF16),
+            pltpu.VMEM(features.shape, BF16),
+            pltpu.VMEM(weights.shape, BF16),
+            dma((6,)),
             pltpu.VMEM((slots, 8, 8, 8, 128), F32),
             pltpu.VMEM((4, cap, 64, 128), BF16),
             pltpu.VMEM((4, cap, 64, 128), BF16),
@@ -351,19 +441,21 @@
             pltpu.VMEM((2, slots // 2, 192, 128), BF16),
             pltpu.VMEM((slots, 128, 128), BF16),
             pltpu.VMEM((3, 192, 256), F32),
-            pltpu.VMEM((half, 2, size, 128), F32),
-            pltpu.VMEM((half, size, 128), F32),
-            pltpu.VMEM((half, size, 128), F32),
-            pltpu.VMEM((half, size, 128), F32),
-            pltpu.VMEM((n_rx, piece, 128), F32),
-            pltpu.VMEM((n_rx, piece, 128), F32),
-            pltpu.VMEM((n_rx, piece, 128), BF16),
-            dma((4,)), dma((4,)), dma((6, most)),
-            dma((half,)), dma((half,)), dma((n_rx,)), dma((n_rx,)), dma((half,)), dma((half,)),
+            pltpu.VMEM((2, 2, half, unit, 128), F32),
+            pltpu.VMEM((2, half, unit, 128), F32),
+            pltpu.VMEM((2, half, unit, 128), F32),
+            pltpu.VMEM((2, half, unit, 128), F32),
+            pltpu.VMEM((2, unit, 128), F32),
+            pltpu.VMEM((n_rx, unit, 128), F32),
+            dma((4,)), dma((4,)),
+            dma((2,)), dma((2, half)), dma((2,)), dma((n_rx,)), dma((2, half)), dma((2, half)),
+            dma((2,)), dma((2, half)), dma((n_rx,)), dma((2,)), dma((2, half)), dma((2, half)),
         ],
-        compiler_params=pltpu.CompilerParams(collective_id=0, has_side_effects=True),
+        compiler_params=pltpu.CompilerParams(
+            collective_id=0, has_side_effects=True, vmem_limit_bytes=40 << 20
+        ),
         name="main",
-    )(live_count, send_list, neighbor, features, grad_out, weights)
+    )(live_count, *(held(x) for x in (send_list, neighbor, features, grad_out, weights)))
 
     grad_weights, output, grad_features = pl.pallas_call(
         finish_kernel,
@@ -373,7 +465,9 @@
             jax.ShapeDtypeStruct(features.shape, BF16),
         ),
         in_specs=[vmem, vmem, vmem],
-        out_specs=(vmem, vmem, vmem),
+        out_specs=(hbm, hbm, hbm),
+        scratch_shapes=[pltpu.VMEM((27, channels, channels), F32), dma((5,))],
+        compiler_params=pltpu.CompilerParams(vmem_limit_bytes=8 << 20),
         name="finish",
     )(packed, output, grad_features)
     return output, grad_features, grad_weights

time: 35.4 us -> 30 us (0.85)
  Pallas kernels: 34 us -> 28.6 us
    pallas_call x1, Pallas kernels: 31.4 us -> 27.3 us  [body(): pl.pallas_call(functools.partial(main_kernel, n_rx, n_ry, scale, conv_at)...]
    pallas_call x1, Pallas kernels: 2.61 us -> 1.3 us  [body(): pl.pallas_call(finish_kernel, out_shape=(jax.ShapeDtypeStruct((27, channe...]
where the time goes in v2:
time: 30 us; the launch traced here: 29.9 us
  Pallas kernels  28.6 us (95%)
  between operations  1.29 us (4%)
    pallas_call x1, Pallas kernels, body(): pl.pallas_call(functools.partial(main_kernel, n_rx, n_ry, scale, conv_at)...  27.3 us
    pallas_call x1, Pallas kernels, body(): pl.pallas_call(finish_kernel, out_shape=(jax.ShapeDtypeStruct((27, channe...  1.3 us

profile of v2, /device:TPU:0, one launch (start us, length us, event | category | flops | bytes accessed | tf_op | source)
XLA Modules:
  0.0 29.9 jit_solution(10326532449420696117)
XLA Ops:
  1.3 27.3 %main.1 = (bf16[8,64,512]{2,1,0:T(8,128)(2,1)S(1)}, bf16[8,64,512]{2,1,0:T(8,128)(2,1)S(1)}, bf16[2,2,4,56,128]{4,3,2,1,0:T(8,128)(2,1)S(1)}) custom-call(s32[1]{0:T(128)S(6)} %copy.9.live_hbm, s32[4,4]{1,0:T(4,128)} %list_hbm.1, s32[8,6]{1,0:T(8,128)} %nb_hbm.1, bf16[8,64,512]{2,1,0:T(8,128)(2,1)} %feat_hbm.1, bf16[8,64,512]{2,1,0:T(8,128)(2,1)} %grad_hbm.1, ...), custom_call_target="tpu_custom_call" | custom-call | tf_op jit(solution)/shard_map/main/pallas_call | solution.py:416
  28.6 1.3 %finish.1 = (f32[27,64,64]{2,1,0:T(8,128)}, bf16[8,64,512]{2,1,0:T(8,128)(2,1)}, bf16[8,64,512]{2,1,0:T(8,128)(2,1)}) custom-call(bf16[2,2,4,56,128]{4,3,2,1,0:T(8,128)(2,1)S(1)} %get-tuple-element.9.packed_ref, bf16[8,64,512]{2,1,0:T(8,128)(2,1)S(1)} %get-tuple-element.10.out_ref, bf16[8,64,512]{2,1,0:T(8,128)(2,1)S(1)} %get-tuple-element.11.gf_ref), custom_call_target="tpu_custom_call" | custom-call | tf_op jit(solution)/shard_map/finish/pallas_call | solution.py:460
